TPU v7x, 32 devices: a whole 2x2x4 slice. The times are simulated.
32 devices in a mesh: groups: 2 (over x), ctx: 8 (over z, y), tp: 2 (over core).
Axes of the slice: x: 2, y: 2, z: 4, core: 2. Of those that a mesh axis runs over, the one named last changes fastest.
Arguments:
- enc_input: bfloat16 [2048, 4096], P(('groups', 'ctx')), parts along dimension 0, may hold values from -6 to 6
- enc_query: bfloat16 [2048, 1024], P(('groups', 'ctx'), 'tp'), parts along dimension 0
- enc_key: bfloat16 [2048, 1024], P(('groups', 'ctx'), 'tp'), parts along dimension 0
- enc_value: bfloat16 [2048, 1024], P(('groups', 'ctx'), 'tp'), parts along dimension 0, may hold values from -6 to 6
- seq_length: int32 [2], P('groups'), parts along dimension 0, may hold values from 256 to 1024
- attn_out_weight: bfloat16 [1024, 4096], P('tp'), may hold values from -0.1875 to 0.1875
- enc_gain: bfloat16 [4096], replicated, may hold values from 0.25 to 1.75
- cross_key_weight: bfloat16 [4096, 1024], P('ctx', 'tp'), may hold values from -0.09375 to 0.09375
- cross_value_weight: bfloat16 [4096, 1024], P('ctx', 'tp'), may hold values from -0.09375 to 0.09375
- embed_table: bfloat16 [32128, 4096], P('tp', 'ctx')
- dec_ids: int32 [32, 2], P('groups'), parts along dimension 0, may hold values from 0 to 32127
- dec_gain: bfloat16 [4096], P('ctx'), may hold values from 0.25 to 1.75
- cross_query_weight: bfloat16 [4096, 1024], P('ctx', 'tp')
- cross_out_weight: bfloat16 [1024, 4096], P('tp', 'ctx'), may hold values from -0.1875 to 0.1875
Outputs:
- cross_keys: bfloat16 [16, 128, 1024], P(('groups', 'ctx'), None, 'tp'), parts along dimension 0
- cross_values: bfloat16 [16, 128, 1024], P(('groups', 'ctx'), None, 'tp'), parts along dimension 0
- decoded: bfloat16 [32, 2, 4096], P('groups', None, 'ctx'), parts along dimension 0
There are 2 independent parts, one for each index of `groups`. A program takes and returns all parts, laid end to end along the dimension named above; an argument that names none is the same for every part. Nothing has to cross between parts.
Inputs may be any that keep to these rules, and one draw needn't show every extreme that they name: `seq_length`: the input's real length.
All inputs are finite; a program needn't handle non-finite values.
Results may differ from a plain program's by a relative error of at most 0.04.
Values may be sent and summed in bfloat16 or wider, within the bound.
A program may use at most 128 MiB of HBM per device.

v0:
```python
import math
import jax
import jax.numpy as jnp
from jax import lax
from jax.sharding import PartitionSpec as P

D = 4096
HD = 128
EPSILON = 1e-06
FLOOR = -1e30


def joined(value, axis, join):
    pieces = jax.tree.map(lambda part: lax.all_gather(part, axis), value)
    head = jax.tree.map(lambda part: part[0], pieces)
    tail = jax.tree.map(lambda part: part[1:], pieces)
    total, _ = lax.scan(lambda total, piece: (join(total, piece), None), head, tail)
    return total


def softmax_merge(first, second):
    top_first, total_first, mixed_first = first
    top_second, total_second, mixed_second = second
    top = jnp.maximum(top_first, top_second)
    weight_first = jnp.exp(top_first - top)
    weight_second = jnp.exp(top_second - top)
    total = total_first * weight_first + total_second * weight_second
    mixed = mixed_first * weight_first[..., None] + mixed_second * weight_second[..., None]
    return (top, total, mixed)


def partial_softmax(queries, keys, values, valid, factor):
    scores = jnp.einsum("qhd,khd->hqk", queries, keys, preferred_element_type=jnp.float32) * factor
    scores = jnp.where(valid[None, None, :], scores, FLOOR)
    top = jnp.max(scores, axis=-1)
    probs = jnp.where(valid[None, None, :], jnp.exp(scores - top[..., None]), 0.0)
    total = jnp.sum(probs, axis=-1)
    mixed = jnp.einsum(
        "hqk,khd->hqd", probs.astype(jnp.bfloat16), values, preferred_element_type=jnp.float32
    )
    return (top, total, mixed)


def norm_rows(resid, gain):
    scale = lax.rsqrt(jnp.mean(resid * resid, axis=-1, keepdims=True) + EPSILON)
    return (resid * scale * gain.astype(jnp.float32)).astype(jnp.bfloat16)


def local(
    enc_input,
    enc_query,
    enc_key,
    enc_value,
    seq_length,
    attn_out_weight,
    enc_gain,
    cross_key_weight,
    cross_value_weight,
    embed_table,
    dec_ids,
    dec_gain,
    cross_query_weight,
    cross_out_weight,
):
    rows, inner_local = enc_query.shape
    heads_local = inner_local // HD
    limit = seq_length[0]
    queries = enc_query.reshape(rows, heads_local, HD)
    start_state = (
        jnp.full((heads_local, rows), FLOOR, jnp.float32),
        jnp.zeros((heads_local, rows), jnp.float32),
        jnp.zeros((heads_local, rows, HD), jnp.float32),
    )
    carry = start_state
    key_rows = lax.all_gather(enc_key, "ctx", axis=0, tiled=True)
    value_rows = lax.all_gather(enc_value, "ctx", axis=0, tiled=True)
    count = key_rows.shape[0]
    block = math.gcd(count, 2048)
    blocks = count // block
    key_blocks = key_rows.reshape(blocks, block, heads_local, HD)
    value_blocks = value_rows.reshape(blocks, block, heads_local, HD)
    offsets = jnp.arange(blocks, dtype=jnp.int32) * block

    def one_block(state, item):
        key_block, value_block, offset = item
        positions = offset + jnp.arange(block, dtype=jnp.int32)
        update = partial_softmax(queries, key_block, value_block, positions < limit, HD ** (-0.5))
        return (softmax_merge(state, update), None)

    carry, unused = lax.scan(one_block, carry, (key_blocks, value_blocks, offsets))
    top, total, mixed = carry
    context = (
        jnp.transpose(mixed / total[..., None], (1, 0, 2))
        .reshape(rows, inner_local)
        .astype(jnp.bfloat16)
    )
    summed = lax.psum(jnp.dot(context, attn_out_weight, preferred_element_type=jnp.float32), "tp")
    memory = norm_rows(enc_input.astype(jnp.float32) + summed, enc_gain)
    ctx_count = lax.axis_size("ctx")
    slots = rows // ctx_count
    key_sum = jnp.dot(
        memory,
        lax.all_gather(cross_key_weight, "ctx", axis=0, tiled=True),
        preferred_element_type=jnp.float32,
    )
    value_sum = jnp.dot(
        memory,
        lax.all_gather(cross_value_weight, "ctx", axis=0, tiled=True),
        preferred_element_type=jnp.float32,
    )
    key_rows = key_sum.astype(jnp.bfloat16)
    value_rows = value_sum.astype(jnp.bfloat16)
    keys_moved, values_moved = (
        lax.all_to_all(
            key_rows.reshape(slots, ctx_count, inner_local),
            "ctx",
            split_axis=1,
            concat_axis=0,
            tiled=True,
        ),
        lax.all_to_all(
            value_rows.reshape(slots, ctx_count, inner_local),
            "ctx",
            split_axis=1,
            concat_axis=0,
            tiled=True,
        ),
    )
    keys_cache = keys_moved.reshape(rows, inner_local)
    values_cache = values_moved.reshape(rows, inner_local)
    beams = dec_ids.shape[0]
    vocab_local = embed_table.shape[0]
    flat_ids = dec_ids.reshape(-1) - lax.axis_index("tp") * vocab_local
    inside = (flat_ids >= 0) & (flat_ids < vocab_local)
    looked = jnp.take(embed_table, jnp.clip(flat_ids, 0, vocab_local - 1), axis=0)
    own_rows = jnp.where(inside[:, None], looked.astype(jnp.float32), 0.0)
    hidden = lax.psum(own_rows.astype(jnp.bfloat16), "tp").astype(jnp.float32)
    scaled = (hidden * dec_gain.astype(jnp.float32)).astype(jnp.bfloat16)
    raw_part = jnp.dot(scaled, cross_query_weight, preferred_element_type=jnp.float32)
    square_part = jnp.sum(hidden * hidden, axis=-1)
    raw, squares = lax.psum((raw_part, square_part), "ctx")
    factor = lax.rsqrt(squares / D + EPSILON)
    query = (raw * factor[:, None] * HD ** (-0.5)).astype(jnp.bfloat16).reshape(-1, heads_local, HD)
    positions = jnp.arange(rows, dtype=jnp.int32) * ctx_count + lax.axis_index("ctx")
    local_part = partial_softmax(
        query,
        keys_cache.reshape(rows, heads_local, HD),
        values_cache.reshape(rows, heads_local, HD),
        positions < limit,
        1.0,
    )
    top_all, total_all, mixed_all = joined(local_part, "ctx", softmax_merge)
    attn = (
        jnp.transpose(mixed_all / total_all[..., None], (1, 0, 2))
        .reshape(-1, inner_local)
        .astype(jnp.bfloat16)
    )
    out_part = jnp.dot(attn, cross_out_weight, preferred_element_type=jnp.float32)
    out = lax.psum(out_part, "tp")
    decoded = (out + hidden).astype(jnp.bfloat16).reshape(beams, 2, -1)
    return (keys_cache[None], values_cache[None], decoded)


def solution(mesh):
    placed = (
        P(("groups", "ctx"), None),
        P(("groups", "ctx"), "tp"),
        P(("groups", "ctx"), "tp"),
        P(("groups", "ctx"), "tp"),
        P("groups"),
        P("tp", None),
        P(),
        P("ctx", "tp"),
        P("ctx", "tp"),
        P("tp", "ctx"),
        P("groups", None),
        P("ctx"),
        P("ctx", "tp"),
        P("tp", "ctx"),
    )
    return jax.shard_map(
        local,
        mesh=mesh,
        in_specs=placed,
        out_specs=(
            P(("groups", "ctx"), None, "tp"),
            P(("groups", "ctx"), None, "tp"),
            P("groups", None, "ctx"),
        ),
        check_vma=False,
    )
```

profile of v0, /device:TPU:0, one launch (start us, length us, event | category | flops | bytes accessed | tf_op | source)
XLA Modules:
  0.0 454.3 jit_solution(15801881285562292397)
XLA Ops:
  7.2 0.0 all-gather.10.cloned.1.call-start
  7.2 1.7 copy.38
  9.0 0.0 all-gather.12.cloned.1.call-start
  9.0 0.7 all-gather.12.cloned.1.call-update
  9.7 0.0 all-reduce.4.cloned.1.call-start
  10.4 42.3 %all-gather.10.cloned.1.call-done = bf16[1024,512]{0,1:T(8,128)(2,1)} async-done(((bf16[128,512]{0,1:T(8,128)(2,1)}), bf16[1024,512]{0,1:T(8,128)(2,1)}) %all-gather.10.cloned.1.call-update) | async-done | bytes 1048592 | tf_op jit(solution)/shard_map/all_gather | solution.py:75
  52.8 1.9 fusion.3
  54.6 0.6 fusion.4
  55.2 39.0 %all-gather.12.cloned.1.call-done = bf16[1024,512]{1,0:T(8,128)(2,1)} async-done(((bf16[128,512]{1,0:T(8,128)(2,1)}), bf16[1024,512]{1,0:T(8,128)(2,1)}) %all-gather.12.cloned.1.call-update) | async-done | bytes 1048592 | tf_op jit(solution)/shard_map/all_gather | solution.py:76
  94.2 2.3 copy.41
  96.5 2.1 fusion.9
  98.6 0.4 copy-done.3
  99.0 2.1 fusion.54
  101.1 0.0 all-reduce.4.cloned.1.call-update
  101.1 0.0 all-gather.14.cloned.1.call-start
  101.1 0.5 all-gather.14.cloned.1.call-update
  101.7 0.0 all-gather.16.cloned.1.call-start
  101.7 0.5 all-gather.16.cloned.1.call-update
  102.3 0.0 all-reduce.6.cloned.1.call-start
  102.3 0.1 copy.45
  102.4 0.1 min.18
  102.5 0.1 min.16
  102.6 0.1 copy.44
  102.7 0.1 and.20
  102.8 9.3 %gather_fusion = bf16[32,512]{1,0:T(8,128)(2,1)S(1)} fusion(bf16[16064,512]{1,0:T(8,128)(2,1)} %param.25, s32[1024]{0:T(1024)S(1)} %pad_clamp_fusion), kind=kCustom, calls=%fused_computation | custom fusion | bytes 65664 | tf_op jit(solution)/shard_map/jit(_take)/gather | solution.py:135
  112.2 0.1 select_convert_fusion
  112.3 3.4 psum.36
  115.7 0.8 fusion.31
  116.5 0.1 fusion.25
  116.7 18.3 %psum.38 = f32[32]{0:T(128)S(1)} all-reduce(f32[32]{0:T(128)S(1)} %fusion.25), channel_id=1, replica_groups=mesh['groups'=2,'ctx'=8,'tp'=2] {'ctx'}, use_global_device_ids=true, to_apply=%region_7.8 | all-reduce | flops 32 | bytes 256 | tf_op jit(solution)/shard_map/psum | solution.py:141
  135.0 2.1 multiply_reduce_fusion
  137.1 0.1 copy-done.1
  137.2 0.4 multiply_convert_fusion
  137.6 59.6 %all-gather.14.cloned.1.call-done = bf16[4096,512]{1,0:T(8,128)(2,1)} async-done(((bf16[512,512]{1,0:T(8,128)(2,1)}), bf16[4096,512]{1,0:T(8,128)(2,1)}) %all-gather.14.cloned.1.call-update) | async-done | bytes 4194320 | tf_op jit(solution)/shard_map/all_gather | solution.py:103
  197.2 2.9 fusion.10
  200.2 0.7 copy.42
  200.9 3.4 all-to-all-start
  204.2 66.7 %all-gather.16.cloned.1.call-done = bf16[4096,512]{1,0:T(8,128)(2,1)} async-done(((bf16[512,512]{1,0:T(8,128)(2,1)}), bf16[4096,512]{1,0:T(8,128)(2,1)}) %all-gather.16.cloned.1.call-update) | async-done | bytes 4194320 | tf_op jit(solution)/shard_map/all_gather | solution.py:108
  271.0 2.9 fusion.11
  273.9 0.7 copy.43
  274.6 3.4 all-to-all-start.1
  278.0 0.0 all-reduce.8.cloned.1.call-start
  278.1 7.3 %all-to-all-done.1 = bf16[16,8,512]{2,0,1:T(8,128)(2,1)S(1)} async-done(((bf16[16,8,512]{2,0,1:T(8,128)(2,1)}), bf16[16,8,512]{2,0,1:T(8,128)(2,1)S(1)}, u32[]{:S(2)}, u32[]{:S(2)}) %all-to-all-start.1) | async-done | bytes 131104 | tf_op jit(solution)/shard_map/all_to_all | solution.py:121
  285.4 56.9 %all-reduce.6.cloned.1.call-done = f32[32,512]{1,0:T(8,128)} async-done(((f32[32,512]{1,0:T(8,128)}), f32[32,512]{1,0:T(8,128)}) %all-reduce.6.cloned.1.call-update) | async-done | bytes 65552 | tf_op jit(solution)/shard_map/psum | solution.py:141
  342.3 1.1 fusion.53
  343.4 0.2 fusion.21
  343.7 31.4 %all-gather.2 = f32[32,32,128]{2,1,0:T(8,128)S(1)} all-gather(f32[4,32,128]{2,1,0:T(8,128)S(1)} %fusion.21), channel_id=4, replica_groups=mesh['groups'=2,'ctx'=8,'tp'=2] {'ctx'}, dimensions={0}, use_global_device_ids=true | all-gather | bytes 589824 | tf_op jit(solution)/shard_map/all_gather | solution.py:14
  375.1 0.2 fusion.28
  375.3 26.1 %all-gather.4 = f32[8,4,32]{2,1,0:T(4,128)S(1)} all-gather(f32[1,4,32]{2,1,0:T(4,128)S(1)} %bitcast.122), channel_id=3, replica_groups=mesh['groups'=2,'ctx'=8,'tp'=2] {'ctx'}, dimensions={0}, use_global_device_ids=true | all-gather | bytes 4608 | tf_op jit(solution)/shard_map/all_gather | solution.py:14
  401.4 26.1 %all-gather.3 = f32[8,4,32]{2,1,0:T(4,128)S(1)} all-gather(f32[1,4,32]{2,1,0:T(4,128)S(1)} %bitcast.121), channel_id=2, replica_groups=mesh['groups'=2,'ctx'=8,'tp'=2] {'ctx'}, dimensions={0}, use_global_device_ids=true | all-gather | bytes 4608 | tf_op jit(solution)/shard_map/all_gather | solution.py:14
  427.6 1.1 while.2
  427.6 0.1 fusion.73
  427.7 0.1 fusion.73
  427.9 0.1 fusion.73
  428.1 0.1 fusion.73
  428.2 0.1 fusion.73
  428.4 0.1 fusion.73
  428.5 0.1 fusion.73
  428.7 0.9 fusion.33
  429.6 15.1 %all-reduce.8.cloned.1.call-done = f32[32,512]{1,0:T(8,128)} async-done(((f32[32,512]{1,0:T(8,128)}), f32[32,512]{1,0:T(8,128)}) %all-reduce.8.cloned.1.call-update) | async-done | bytes 65552 | tf_op jit(solution)/shard_map/psum | solution.py:159
  444.7 0.8 fusion.26
  445.5 0.6 reshape.129
  446.2 0.7 copy.97
  446.8 0.7 copy.98
  (46 shorter events, 0.5 us)
Async XLA Ops:
  7.2 108.5 %copy-start = (bf16[512,512]{1,0:T(8,128)(2,1)S(1)}, bf16[512,512]{1,0:T(8,128)(2,1)}, u32[]{:S(2)}) copy-start(bf16[512,512]{1,0:T(8,128)(2,1)} %param.28) | copy-start | bytes 1572868
  7.2 45.6 %all-gather.10.cloned.1.call-start = ((), (), s32[]{:S(2)}) async-start(), calls=%async_computation.2 | async-start | bytes 1179648 | tf_op jit(solution)/shard_map/all_gather | solution.py:75
  9.0 85.2 %all-gather.12.cloned.1.call-start = ((), (), s32[]{:S(2)}) async-start(), calls=%async_computation.3 | async-start | bytes 1179648 | tf_op jit(solution)/shard_map/all_gather | solution.py:76
  9.7 125.3 %all-reduce.4.cloned.1.call-start = ((), (), s32[]{:S(2)}) async-start(), calls=%async_computation.4 | async-start | bytes 4194304 | tf_op jit(solution)/shard_map/psum | solution.py:97
  96.5 2.5 copy-start.3
  101.0 1.3 copy-start.6
  101.1 1.8 copy-start.7
  101.1 15.6 %copy-start.5 = (bf16[4096]{0:T(1024)(128)(2,1)S(1)}, bf16[4096]{0:T(1024)(128)(2,1)}, u32[]{:S(2)}) copy-start(bf16[4096]{0:T(1024)(128)(2,1)} %param.22) | copy-start | bytes 24580
  101.1 34.0 %copy-start.2 = (bf16[128,4096]{1,0:T(8,128)(2,1)S(1)}, bf16[128,4096]{1,0:T(8,128)(2,1)}, u32[]{:S(2)}) copy-start(bf16[128,4096]{1,0:T(8,128)(2,1)} %param.16) | copy-start | bytes 3145732
  101.1 96.2 %all-gather.14.cloned.1.call-start = ((), (), s32[]{:S(2)}) async-start(), calls=%async_computation.5 | async-start | bytes 4718592 | tf_op jit(solution)/shard_map/all_gather | solution.py:103
  101.7 169.3 %all-gather.16.cloned.1.call-start = ((), (), s32[]{:S(2)}) async-start(), calls=%async_computation.6 | async-start | bytes 4718592 | tf_op jit(solution)/shard_map/all_gather | solution.py:108
  102.3 240.0 %all-reduce.6.cloned.1.call-start = ((), (), s32[]{:S(2)}) async-start(), calls=%async_computation.7 | async-start | bytes 131072 | tf_op jit(solution)/shard_map/psum | solution.py:141
  135.0 2.2 copy-start.1
  200.9 73.7 %all-to-all-start = ((bf16[16,8,512]{2,0,1:T(8,128)(2,1)}), bf16[16,8,512]{2,0,1:T(8,128)(2,1)S(1)}, u32[]{:S(2)}, u32[]{:S(2)}) async-start(bf16[16,8,512]{2,0,1:T(8,128)(2,1)} %copy.42), calls=%async_computation | async-start | bytes 262144 | tf_op jit(solution)/shard_map/all_to_all | solution.py:114
  274.6 10.8 %all-to-all-start.1 = ((bf16[16,8,512]{2,0,1:T(8,128)(2,1)}), bf16[16,8,512]{2,0,1:T(8,128)(2,1)S(1)}, u32[]{:S(2)}, u32[]{:S(2)}) async-start(bf16[16,8,512]{2,0,1:T(8,128)(2,1)} %copy.43), calls=%async_computation.1 | async-start | bytes 262144 | tf_op jit(solution)/shard_map/all_to_all | solution.py:121
  278.0 150.7 %copy-start.4 = (bf16[512,512]{1,0:T(8,128)(2,1)S(1)}, bf16[512,512]{1,0:T(8,128)(2,1)}, u32[]{:S(2)}) copy-start(bf16[512,512]{1,0:T(8,128)(2,1)} %param.29) | copy-start | bytes 1572868
  278.0 166.7 %all-reduce.8.cloned.1.call-start = ((), (), s32[]{:S(2)}) async-start(), calls=%async_computation.8 | async-start | bytes 131072 | tf_op jit(solution)/shard_map/psum | solution.py:159
Sparse Core Ops, SparseCore 0:
  10.6 42.1 all-gather.9
  54.9 39.2 all-gather.11
  101.2 20.0 all-reduce.3
  123.2 73.9 all-gather.13
  199.2 71.7 all-gather.15
  274.2 68.0 all-reduce.5
  429.7 14.9 all-reduce.7
where the time goes:
time: 455 us; the launch traced here: 454 us
  waiting for transfers between devices  289 us (64%)
  blocking collectives  105 us (23%)
  local copies, waits for them, and re-layouts  17.7 us (4%)
  between operations  15 us (3%)
  matrix products  14.9 us (3%)
  starting transfers between devices  7.02 us (2%)
  other arithmetic  5.36 us (1%)
    all_gather x3, blocking collectives, joined(): pieces = jax.tree.map(lambda part: lax.all_gather(part, axis), value)  83.7 us
    all_gather x1, waiting for transfers between devices, local(): lax.all_gather(cross_value_weight, 'ctx', axis=0, tiled=True)  66.7 us
    all_gather x1, waiting for transfers between devices, local(): lax.all_gather(cross_key_weight, 'ctx', axis=0, tiled=True)  59.6 us
    psum x1, waiting for transfers between devices, local(): raw, squares = lax.psum((raw_part, square_part), 'ctx')  56.9 us
    all_gather x1, waiting for transfers between devices, local(): key_rows = lax.all_gather(enc_key, 'ctx', axis=0, tiled=True)  42.3 us
    all_gather x1, waiting for transfers between devices, local(): value_rows = lax.all_gather(enc_value, 'ctx', axis=0, tiled=True)  39 us
    psum x1, blocking collectives, local(): raw, squares = lax.psum((raw_part, square_part), 'ctx')  18.3 us
    psum x1, waiting for transfers between devices, local(): out = lax.psum(out_part, 'tp')  15.1 us
  transfers between devices with their start and end apart: 9, of which 7 were waited for; matrix products, arithmetic and copies ran while one was open for 5% of the time, Pallas kernels for 0%

commit v1 on v0

--- a/solution.py
+++ b/solution.py
@@ -73,7 +73,9 @@
     )
     carry = start_state
     key_rows = lax.all_gather(enc_key, "ctx", axis=0, tiled=True)
-    value_rows = lax.all_gather(enc_value, "ctx", axis=0, tiled=True)
+    value_rows = jnp.concatenate(
+        lax.all_to_all(jnp.stack([enc_value] * lax.axis_size("ctx")), "ctx", 0, 0), axis=0
+    )
     count = key_rows.shape[0]
     block = math.gcd(count, 2048)
     blocks = count // block

time: 455 us -> 429 us (0.943)
  waiting for transfers between devices: 289 us -> 251 us
  starting transfers between devices: 7.02 us -> 14.3 us
  local copies, waits for them, and re-layouts: 17.7 us -> 22.8 us
    all_gather x1 -> x0, waiting for transfers between devices: 39 us -> none  [local(): value_rows = lax.all_gather(enc_value, 'ctx', axis=0, tiled=True)]
    all_to_all x0 -> x1, starting transfers between devices: none -> 7.31 us  [local(): lax.all_to_all(jnp.stack([enc_value] * lax.axis_size('ctx')), 'ctx', 0, 0)]
  transfers between devices with their start and end apart: 9 -> 9, of which waited for: 7 -> 6; matrix products, arithmetic and copies ran while one was open for 5% -> 6% of each run, Pallas kernels for 0% -> 0%
where the time goes in v1:
time: 429 us
  waiting for transfers between devices  251 us (59%)
  blocking collectives  106 us (25%)
  local copies, waits for them, and re-layouts  22.8 us (5%)
  between operations  15.1 us (4%)
  matrix products  14.8 us (3%)
  starting transfers between devices  14.3 us (3%)
  other arithmetic  5.36 us (1%)
    all_gather x3, blocking collectives, joined(): pieces = jax.tree.map(lambda part: lax.all_gather(part, axis), value)  83.7 us
    all_gather x1, waiting for transfers between devices, local(): lax.all_gather(cross_value_weight, 'ctx', axis=0, tiled=True)  66.8 us
    all_gather x1, waiting for transfers between devices, local(): lax.all_gather(cross_key_weight, 'ctx', axis=0, tiled=True)  59.8 us
    psum x1, waiting for transfers between devices, local(): raw, squares = lax.psum((raw_part, square_part), 'ctx')  56.9 us
    all_gather x1, waiting for transfers between devices, local(): key_rows = lax.all_gather(enc_key, 'ctx', axis=0, tiled=True)  43.5 us
    psum x1, blocking collectives, local(): raw, squares = lax.psum((raw_part, square_part), 'ctx')  18.5 us
    psum x1, waiting for transfers between devices, local(): out = lax.psum(out_part, 'tp')  15.1 us
    gather x1, local copies, waits for them, and re-layouts, local(): jnp.take(embed_table, jnp.clip(flat_ids, 0, vocab_local - 1), axis=0)  9.27 us
  transfers between devices with their start and end apart: 9, of which 6 were waited for; matrix products, arithmetic and copies ran while one was open for 6% of the time, Pallas kernels for 0%

profile of v1, /device:TPU:0, one launch (start us, length us, event | category | flops | bytes accessed | tf_op | source)
XLA Modules:
  0.0 428.5 jit_solution(1043747916645266064)
XLA Ops:
  7.2 0.0 all-gather.9.cloned.1.call-start
  7.2 1.7 copy.38
  9.0 1.0 copy.41
  10.0 1.1 stack.2
  11.1 7.3 %all-to-all-start = ((bf16[8,128,512]{1,2,0:T(8,128)(2,1)}), bf16[8,128,512]{1,2,0:T(8,128)(2,1)}, u32[]{:S(2)}, u32[]{:S(2)}) async-start(bf16[8,128,512]{1,2,0:T(8,128)(2,1)} %stack.2), calls=%async_computation | async-start | bytes 2097152 | tf_op jit(solution)/shard_map/all_to_all | solution.py:77
  18.5 0.0 all-reduce.4.cloned.1.call-start
  19.2 43.5 %all-gather.9.cloned.1.call-done = bf16[1024,512]{0,1:T(8,128)(2,1)} async-done(((bf16[128,512]{0,1:T(8,128)(2,1)}), bf16[1024,512]{0,1:T(8,128)(2,1)}) %all-gather.9.cloned.1.call-update) | async-done | bytes 1048592 | tf_op jit(solution)/shard_map/all_gather | solution.py:75
  62.6 1.8 fusion.3
  64.4 0.6 fusion.4
  65.0 2.9 copy.42
  68.0 2.3 squeeze.37
  70.3 2.1 fusion.9
  72.4 0.4 copy-done.3
  72.8 2.1 fusion.54
  74.9 0.0 all-gather.11.cloned.1.call-start
  74.9 0.7 all-gather.11.cloned.1.call-update
  75.6 0.0 all-gather.13.cloned.1.call-start
  75.7 0.5 all-gather.13.cloned.1.call-update
  76.2 0.0 all-reduce.6.cloned.1.call-start
  76.3 0.1 copy.46
  76.3 0.1 min.18
  76.4 0.1 min.16
  76.5 0.1 copy.45
  76.6 0.1 and.20
  76.8 9.3 %gather_fusion = bf16[32,512]{1,0:T(8,128)(2,1)S(1)} fusion(bf16[16064,512]{1,0:T(8,128)(2,1)} %param.25, s32[1024]{0:T(1024)S(1)} %pad_clamp_fusion), kind=kCustom, calls=%fused_computation | custom fusion | bytes 65664 | tf_op jit(solution)/shard_map/jit(_take)/gather | solution.py:137
  86.1 0.1 select_convert_fusion
  86.2 3.4 psum.36
  89.6 0.8 fusion.31
  90.4 0.1 fusion.25
  90.6 18.5 %psum.38 = f32[32]{0:T(128)S(1)} all-reduce(f32[32]{0:T(128)S(1)} %fusion.25), channel_id=1, replica_groups=mesh['groups'=2,'ctx'=8,'tp'=2] {'ctx'}, use_global_device_ids=true, to_apply=%region_7.8 | all-reduce | flops 32 | bytes 256 | tf_op jit(solution)/shard_map/psum | solution.py:143
  109.0 2.1 multiply_reduce_fusion
  111.1 0.1 copy-done.1
  111.3 0.4 multiply_convert_fusion
  111.7 59.8 %all-gather.11.cloned.1.call-done = bf16[4096,512]{1,0:T(8,128)(2,1)} async-done(((bf16[512,512]{1,0:T(8,128)(2,1)}), bf16[4096,512]{1,0:T(8,128)(2,1)}) %all-gather.11.cloned.1.call-update) | async-done | bytes 4194320 | tf_op jit(solution)/shard_map/all_gather | solution.py:105
  171.5 2.9 fusion.10
  174.4 0.7 copy.43
  175.1 3.4 all-to-all-start.1
  178.5 66.8 %all-gather.13.cloned.1.call-done = bf16[4096,512]{1,0:T(8,128)(2,1)} async-done(((bf16[512,512]{1,0:T(8,128)(2,1)}), bf16[4096,512]{1,0:T(8,128)(2,1)}) %all-gather.13.cloned.1.call-update) | async-done | bytes 4194320 | tf_op jit(solution)/shard_map/all_gather | solution.py:110
  245.2 2.9 fusion.11
  248.1 0.7 copy.44
  248.8 3.4 all-to-all-start.2
  252.2 0.0 all-reduce.8.cloned.1.call-start
  252.3 7.3 %all-to-all-done.2 = bf16[16,8,512]{2,0,1:T(8,128)(2,1)S(1)} async-done(((bf16[16,8,512]{2,0,1:T(8,128)(2,1)}), bf16[16,8,512]{2,0,1:T(8,128)(2,1)S(1)}, u32[]{:S(2)}, u32[]{:S(2)}) %all-to-all-start.2) | async-done | bytes 131104 | tf_op jit(solution)/shard_map/all_to_all | solution.py:123
  259.6 56.9 %all-reduce.6.cloned.1.call-done = f32[32,512]{1,0:T(8,128)} async-done(((f32[32,512]{1,0:T(8,128)}), f32[32,512]{1,0:T(8,128)}) %all-reduce.6.cloned.1.call-update) | async-done | bytes 65552 | tf_op jit(solution)/shard_map/psum | solution.py:143
  316.5 1.1 fusion.53
  317.7 0.2 fusion.21
  317.9 31.4 %all-gather.2 = f32[32,32,128]{2,1,0:T(8,128)S(1)} all-gather(f32[4,32,128]{2,1,0:T(8,128)S(1)} %fusion.21), channel_id=4, replica_groups=mesh['groups'=2,'ctx'=8,'tp'=2] {'ctx'}, dimensions={0}, use_global_device_ids=true | all-gather | bytes 589824 | tf_op jit(solution)/shard_map/all_gather | solution.py:14
  349.4 0.2 fusion.28
  349.5 26.1 %all-gather.4 = f32[8,4,32]{2,1,0:T(4,128)S(1)} all-gather(f32[1,4,32]{2,1,0:T(4,128)S(1)} %bitcast.122), channel_id=3, replica_groups=mesh['groups'=2,'ctx'=8,'tp'=2] {'ctx'}, dimensions={0}, use_global_device_ids=true | all-gather | bytes 4608 | tf_op jit(solution)/shard_map/all_gather | solution.py:14
  375.7 26.1 %all-gather.3 = f32[8,4,32]{2,1,0:T(4,128)S(1)} all-gather(f32[1,4,32]{2,1,0:T(4,128)S(1)} %bitcast.121), channel_id=2, replica_groups=mesh['groups'=2,'ctx'=8,'tp'=2] {'ctx'}, dimensions={0}, use_global_device_ids=true | all-gather | bytes 4608 | tf_op jit(solution)/shard_map/all_gather | solution.py:14
  401.8 1.1 while.2
  401.8 0.1 fusion.73
  402.0 0.1 fusion.73
  402.1 0.1 fusion.73
  402.3 0.1 fusion.73
  402.5 0.1 fusion.73
  402.6 0.1 fusion.73
  402.8 0.1 fusion.73
  402.9 0.9 fusion.33
  403.8 15.1 %all-reduce.8.cloned.1.call-done = f32[32,512]{1,0:T(8,128)} async-done(((f32[32,512]{1,0:T(8,128)}), f32[32,512]{1,0:T(8,128)}) %all-reduce.8.cloned.1.call-update) | async-done | bytes 65552 | tf_op jit(solution)/shard_map/psum | solution.py:161
  418.9 0.8 fusion.26
  419.8 0.6 reshape.130
  420.4 0.7 copy.98
  421.0 0.7 copy.99
  (50 shorter events, 0.5 us)
Async XLA Ops:
  7.2 82.4 %copy-start = (bf16[512,512]{1,0:T(8,128)(2,1)S(1)}, bf16[512,512]{1,0:T(8,128)(2,1)}, u32[]{:S(2)}) copy-start(bf16[512,512]{1,0:T(8,128)(2,1)} %param.28) | copy-start | bytes 1572868
  7.2 55.4 %copy-start.5 = (bf16[128,512]{1,0:T(8,128)(2,1)S(1)}, bf16[128,512]{1,0:T(8,128)(2,1)}, u32[]{:S(2)}) copy-start(bf16[128,512]{1,0:T(8,128)(2,1)} %param.17) | copy-start | bytes 393220
  7.2 55.4 %all-gather.9.cloned.1.call-start = ((), (), s32[]{:S(2)}) async-start(), calls=%async_computation.3 | async-start | bytes 1179648 | tf_op jit(solution)/shard_map/all_gather | solution.py:75
  11.1 53.9 %all-to-all-start = ((bf16[8,128,512]{1,2,0:T(8,128)(2,1)}), bf16[8,128,512]{1,2,0:T(8,128)(2,1)}, u32[]{:S(2)}, u32[]{:S(2)}) async-start(bf16[8,128,512]{1,2,0:T(8,128)(2,1)} %stack.2), calls=%async_computation | async-start | bytes 2097152 | tf_op jit(solution)/shard_map/all_to_all | solution.py:77
  18.5 90.6 %all-reduce.4.cloned.1.call-start = ((), (), s32[]{:S(2)}) async-start(), calls=%async_computation.4 | async-start | bytes 4194304 | tf_op jit(solution)/shard_map/psum | solution.py:99
  70.3 2.5 copy-start.3
  74.8 1.4 copy-start.7
  74.8 1.9 copy-start.8
  74.8 15.7 %copy-start.6 = (bf16[4096]{0:T(1024)(128)(2,1)S(1)}, bf16[4096]{0:T(1024)(128)(2,1)}, u32[]{:S(2)}) copy-start(bf16[4096]{0:T(1024)(128)(2,1)} %param.22) | copy-start | bytes 24580
  74.8 34.2 %copy-start.2 = (bf16[128,4096]{1,0:T(8,128)(2,1)S(1)}, bf16[128,4096]{1,0:T(8,128)(2,1)}, u32[]{:S(2)}) copy-start(bf16[128,4096]{1,0:T(8,128)(2,1)} %param.16) | copy-start | bytes 3145732
  74.9 96.6 %all-gather.11.cloned.1.call-start = ((), (), s32[]{:S(2)}) async-start(), calls=%async_computation.5 | async-start | bytes 4718592 | tf_op jit(solution)/shard_map/all_gather | solution.py:105
  75.6 169.6 %all-gather.13.cloned.1.call-start = ((), (), s32[]{:S(2)}) async-start(), calls=%async_computation.6 | async-start | bytes 4718592 | tf_op jit(solution)/shard_map/all_gather | solution.py:110
  76.2 240.3 %all-reduce.6.cloned.1.call-start = ((), (), s32[]{:S(2)}) async-start(), calls=%async_computation.7 | async-start | bytes 131072 | tf_op jit(solution)/shard_map/psum | solution.py:143
  109.0 2.2 copy-start.1
  175.1 73.8 %all-to-all-start.1 = ((bf16[16,8,512]{2,0,1:T(8,128)(2,1)}), bf16[16,8,512]{2,0,1:T(8,128)(2,1)S(1)}, u32[]{:S(2)}, u32[]{:S(2)}) async-start(bf16[16,8,512]{2,0,1:T(8,128)(2,1)} %copy.43), calls=%async_computation.1 | async-start | bytes 262144 | tf_op jit(solution)/shard_map/all_to_all | solution.py:116
  248.8 10.8 %all-to-all-start.2 = ((bf16[16,8,512]{2,0,1:T(8,128)(2,1)}), bf16[16,8,512]{2,0,1:T(8,128)(2,1)S(1)}, u32[]{:S(2)}, u32[]{:S(2)}) async-start(bf16[16,8,512]{2,0,1:T(8,128)(2,1)} %copy.44), calls=%async_computation.2 | async-start | bytes 262144 | tf_op jit(solution)/shard_map/all_to_all | solution.py:123
  252.2 150.7 %copy-start.4 = (bf16[512,512]{1,0:T(8,128)(2,1)S(1)}, bf16[512,512]{1,0:T(8,128)(2,1)}, u32[]{:S(2)}) copy-start(bf16[512,512]{1,0:T(8,128)(2,1)} %param.29) | copy-start | bytes 1572868
  252.2 166.7 %all-reduce.8.cloned.1.call-start = ((), (), s32[]{:S(2)}) async-start(), calls=%async_computation.8 | async-start | bytes 131072 | tf_op jit(solution)/shard_map/psum | solution.py:161
Sparse Core Ops, SparseCore 0:
  10.6 51.9 all-gather.8
  75.0 20.2 all-reduce.3
  97.5 73.9 all-gather.10
  173.5 71.7 all-gather.12
  248.5 68.0 all-reduce.5
  403.9 14.9 all-reduce.7
